TPU v7x, 256 devices: a whole 4x4x8 slice. The times are simulated.
256 devices in a mesh: branch: 32 (over z, y_lo, core), bus: 8 (over x, y_hi).
Axes of the slice: x: 4, y: 4 (y_hi: 2, y_lo: 2; y = y_hi * 2 + y_lo), z: 8, core: 2. Of those that a mesh axis runs over, the one named last changes fastest.
Arguments:
- injections: float32 [512, 60416], P('branch', 'bus'), may hold values from -0.0234375 to 0.0234375
- ptdf_mon: float32 [4096, 60416], P('branch', 'bus'), may hold values from -2.5 to 2.5
- ptdf_out: float32 [2048, 60416], P('branch', 'bus'), may hold values from -2.5 to 2.5
- outage_from: int32 [2048], replicated, may hold values from 0 to 60415
- outage_to: int32 [2048], replicated, may hold values from 0 to 60415
- hour_ids: int32 [512], P('bus'), may hold values from 0 to 8759
- ratings: float32 [4096, 4], P('branch'), may hold values from 0.5 to 2
Outputs:
- worst_loading: float32 [512, 4096], P('bus', 'branch')
All inputs are finite; a program needn't handle non-finite values.
Results may differ from a plain program's by a relative error of at most 0.00019.
Values sent between devices are 32-bit elements; how exact they have to be, the bound alone decides.
A program may use at most 128 MiB of HBM per device.

v0:
```python
import jax
import jax.numpy as jnp
from jax import lax
from jax.sharding import PartitionSpec as P


def screen(base_mon, outage_base, lodf_t, block_size):
    outage_count = lodf_t.shape[0]

    def advance(index, worst_load):
        first = index * block_size
        lodf_block = lax.dynamic_slice_in_dim(lodf_t, first, block_size, 0)
        flow_block = lax.dynamic_slice_in_dim(outage_base, first, block_size, 1)
        after_outage = base_mon[:, None, :] + flow_block[:, :, None] * lodf_block[None, :, :]
        return jnp.maximum(worst_load, jnp.max(jnp.abs(after_outage), axis=1))

    return lax.fori_loop(0, outage_count // block_size, advance, jnp.abs(base_mon))


def on_device(injections, ptdf_mon, ptdf_out, outage_from, outage_to, hour_ids, ratings):
    highest = lax.Precision.HIGHEST
    mon_rows = ptdf_mon.shape[0]
    out_rows = ptdf_out.shape[0]
    bus_width = ptdf_mon.shape[1]
    bus_count = lax.axis_size("bus")
    bus_index = lax.axis_index("bus")
    contract = (((1,), (1,)), ((), ()))
    piece = lax.all_gather(injections, "branch", axis=0, tiled=True)
    monitored = lax.dot_general(
        piece, ptdf_mon, contract, precision=highest, preferred_element_type=jnp.float32
    )
    outaged = lax.dot_general(
        piece, ptdf_out, contract, precision=highest, preferred_element_type=jnp.float32
    )
    partial_flows = jnp.concatenate([monitored, outaged], axis=1)
    hours_dev = partial_flows.shape[0] // bus_count
    summed_flows = lax.psum(partial_flows, "bus")
    base_flows = lax.dynamic_slice_in_dim(summed_flows, bus_index * hours_dev, hours_dev, 0)
    offset = bus_index * bus_width

    def localize(bus_ids):
        shifted = bus_ids - offset
        inside = jnp.logical_and(shifted >= 0, shifted < bus_width).astype(jnp.float32)
        return (jnp.clip(shifted, 0, bus_width - 1), inside)

    from_index, from_inside = localize(outage_from)
    to_index, to_inside = localize(outage_to)

    def columns(matrix):
        return (
            jnp.take(matrix, from_index, axis=1) * from_inside[None, :]
            - jnp.take(matrix, to_index, axis=1) * to_inside[None, :]
        )

    first_outage = lax.axis_index("branch") * out_rows
    sens_mon, sens_out = lax.psum((columns(ptdf_mon), columns(ptdf_out)), "bus")
    self_sens = jnp.diagonal(lax.dynamic_slice_in_dim(sens_out, first_outage, out_rows, 1))
    base_mon = base_flows[:, :mon_rows]
    base_out = base_flows[:, mon_rows:]
    outage_base, outage_self = (
        lax.all_gather(base_out, "branch", axis=1, tiled=True),
        lax.all_gather(self_sens, "branch", axis=0, tiled=True),
    )
    divisor = jnp.maximum(1.0 - outage_self, 0.25)
    lodf_t = (sens_mon / divisor[None, :]).T
    worst_load = screen(base_mon, outage_base, lodf_t, min(256, lodf_t.shape[0]))
    season = hour_ids * 4 // 8760
    onehot = (season[:, None] == jnp.arange(ratings.shape[1], dtype=jnp.int32)[None, :]).astype(
        jnp.float32
    )
    hour_rating = jnp.dot(onehot, ratings.T, precision=highest, preferred_element_type=jnp.float32)
    return worst_load / hour_rating


def solution(mesh):
    placed = (
        P("branch", "bus"),
        P("branch", "bus"),
        P("branch", "bus"),
        P(),
        P(),
        P("bus"),
        P("branch", None),
    )
    return jax.shard_map(
        on_device, mesh=mesh, in_specs=placed, out_specs=P("bus", "branch"), check_vma=False
    )
```

profile of v0, /device:TPU:6, one launch (start us, length us, event | category | flops | bytes accessed | tf_op | source)
XLA Modules:
  0.0 396.1 jit_solution(17618373268766414951)
XLA Ops:
  7.3 5.4 %copy.22 = f32[128,7552]{0,1:T(8,128)} copy(f32[128,7552]{1,0:T(8,128)} %param.14) | data formatting | bytes 7733248 | tf_op args[1]
  12.7 7.6 %gather_fusion.2 = f32[2048,128]{1,0:T(8,128)S(1)} fusion(f32[128,7552]{0,1:T(8,128)} %copy.22, s32[2048]{0:T(1024)S(1)} %get-tuple-element.139), kind=kCustom, calls=%fused_computation.2.clone | custom fusion | bytes 2105344 | tf_op jit(solution)/shard_map/jit(_take)/gather | solution.py:52
  20.3 9.8 %gather_fusion.1 = f32[2048,128]{1,0:T(8,128)} fusion(f32[128,7552]{0,1:T(8,128)} %copy.22, s32[2048]{0:T(1024)S(1)} %get-tuple-element.138), kind=kCustom, calls=%fused_computation.clone | custom fusion | bytes 2105344 | tf_op jit(solution)/shard_map/jit(_take)/gather | solution.py:51
  30.1 2.7 copy.24
  32.9 9.8 %gather_fusion.4 = f32[2048,64]{1,0:T(8,128)} fusion(f32[64,7552]{0,1:T(8,128)} %copy.24, s32[2048]{0:T(1024)S(1)} %get-tuple-element.139), kind=kCustom, calls=%fused_computation.3.clone | custom fusion | bytes 1056768 | tf_op jit(solution)/shard_map/jit(_take)/gather | solution.py:52
  42.7 9.8 %gather_fusion.3 = f32[2048,64]{1,0:T(8,128)} fusion(f32[64,7552]{0,1:T(8,128)} %copy.24, s32[2048]{0:T(1024)S(1)} %get-tuple-element.138), kind=kCustom, calls=%fused_computation.1.clone | custom fusion | bytes 1056768 | tf_op jit(solution)/shard_map/jit(_take)/gather | solution.py:51
  52.5 4.4 %fusion.1 = f32[128,2048]{0,1:T(8,128)} fusion(f32[2048,128]{1,0:T(8,128)S(1)} %gather_fusion.2, f32[2048,128]{1,0:T(8,128)} %gather_fusion.1, f32[2048]{0:T(1024)S(1)} %get-tuple-element.135, f32[2048]{0:T(1024)S(1)} %get-tuple-element.136, pred[2048]{0:T(1024)(128)(4,1)S(1)} %get-tuple-element.134, pred[2048]{0:T(1024)(128)(4,1)S(1)} %get-tuple-element.137), kind=kLoop, calls=%fused_computation.13 | loop fusion | flops 1310720 | bytes 3166208 | tf_op jit(solution)/shard_map/sub | solution.py:51
  56.9 2.9 fusion
  59.8 45.4 %all-gather.2.cloned.1.call-done = f32[512,7552]{1,0:T(8,128)} async-done(((f32[16,7552]{1,0:T(8,128)}), f32[512,7552]{1,0:T(8,128)}) %all-gather.2.cloned.1.call-update) | async-done | bytes 15466512 | tf_op jit(solution)/shard_map/all_gather | solution.py:28
  105.2 19.0 %fusion.7 = f32[512,64]{0,1:T(8,128)S(1)} fusion(f32[512,7552]{1,0:T(8,128)} %all-gather.2.cloned.1.call-done, f32[64,7552]{1,0:T(8,128)S(1)} %copy-done.3), kind=kOutput, calls=%fused_computation.34 | convolution fusion | flops 2969567232 | bytes 17530880 | tf_op jit(solution)/shard_map/dot_general | solution.py:32
  124.3 16.4 %fusion.6 = f32[512,128]{0,1:T(8,128)S(1)} fusion(f32[512,7552]{1,0:T(8,128)S(1)} %copy-done.1, f32[128,7552]{1,0:T(8,128)S(1)} %copy-done.2), kind=kOutput, calls=%fused_computation.33 | convolution fusion | flops 5939134464 | bytes 19595264 | tf_op jit(solution)/shard_map/dot_general | solution.py:29
  142.9 128.5 %all-reduce.4.cloned.1.call-done = (f32[512,192]{0,1:T(8,128)}, f32[128,2048]{0,1:T(8,128)}, f32[64,2048]{0,1:T(8,128)}) async-done(((f32[512,192]{0,1:T(8,128)}, f32[128,2048]{0,1:T(8,128)}, f32[64,2048]{0,1:T(8,128)}), (f32[512,192]{0,1:T(8,128)}, f32[128,2048]{0,1:T(8,128)}, f32[64,2048]{0,1:T(8,128)})) %all-reduce.4.cloned.1.call-update) | async-done | bytes 1966096 | tf_op jit(solution)/shard_map/psum | solution.py:37
  271.4 1.0 fusion.5
  273.4 36.4 %all_gather.10 = f32[64,2048]{0,1:T(8,128)S(1)} all-gather(f32[64,64]{0,1:T(8,128)S(1)} %dynamic-slice.2), channel_id=1, replica_groups=mesh['branch'=32,'bus'=8] {'branch'}, dimensions={1}, use_global_device_ids=true | all-gather | bytes 540672 | tf_op jit(solution)/shard_map/all_gather | solution.py:61
  312.0 54.3 %all-reduce = f32[2048]{0:T(1024)S(1)} all-reduce(f32[2048]{0:T(1024)S(1)} %dynamic-update-slice), channel_id=1, replica_groups=mesh['branch'=32,'bus'=8] {'branch'}, use_global_device_ids=true, to_apply=%add | all-reduce | flops 2048 | bytes 16384
  366.7 21.7 %while.13 = (s32[]{:T(128)}, f32[64,128]{1,0:T(8,128)S(1)}, f32[64,128]{1,0:T(8,128)S(1)}, f32[64,2048]{1,0:T(8,128)S(1)}, f32[2048,128]{1,0:T(8,128)S(1)}, /*index=5*/s32[]{:T(128)}, s32[]{:T(128)}, s32[]{:T(128)}, s32[]{:T(128)}) while((s32[]{:T(128)}, f32[64,128]{1,0:T(8,128)S(1)}, f32[64,128]{1,0:T(8,128)S(1)}, f32[64,2048]{1,0:T(8,128)S(1)}, ...), condition=%wide.region_5.8_spmd, body=%wide.region_3.7_spmd.sunk | while | flops 8388614 | bytes 753819 | solution.py:17
  366.8 2.6 abs_reduce_fusion.2
  369.5 2.6 abs_reduce_fusion.2
  372.2 2.6 abs_reduce_fusion.2
  374.9 2.6 abs_reduce_fusion.2
  377.6 2.6 abs_reduce_fusion.2
  380.3 2.6 abs_reduce_fusion.2
  383.1 2.6 abs_reduce_fusion.2
  385.8 2.6 abs_reduce_fusion.2
  (67 shorter events, 6.9 us)
Async XLA Ops:
  6.5 381.9 %copy-start = (f32[128,4]{0,1:T(4,128)S(1)}, f32[128,4]{0,1:T(4,128)}, u32[]{:S(2)}) copy-start(f32[128,4]{0,1:T(4,128)} %param.19) | copy-start | bytes 6148
  6.5 98.7 %all-gather.2.cloned.1.call-start = ((), (), s32[]{:S(2)}) async-start(), calls=%async_computation | async-start | bytes 15949824 | tf_op jit(solution)/shard_map/all_gather | solution.py:28
  7.3 264.1 %all-reduce.4.cloned.1.call-start = ((), (), s32[]{:S(2)}) async-start(), calls=%async_computation.1 | async-start | bytes 4980736 | tf_op jit(solution)/shard_map/psum | solution.py:37
  7.3 5.4 %copy-start.7 = (s32[2048]{0:T(1024)S(1)}, s32[2048]{0:T(1024)}, u32[]{:S(2)}) copy-start(s32[2048]{0:T(1024)} %param.16) | copy-start | bytes 24580
  7.3 5.4 %copy-start.8 = (s32[2048]{0:T(1024)S(1)}, s32[2048]{0:T(1024)}, u32[]{:S(2)}) copy-start(s32[2048]{0:T(1024)} %param.17) | copy-start | bytes 24580
  20.3 9.9 %copy-start.3 = (f32[64,7552]{1,0:T(8,128)S(1)}, f32[64,7552]{1,0:T(8,128)}, u32[]{:S(2)}) copy-start(f32[64,7552]{1,0:T(8,128)} %param.15) | copy-start | bytes 5799940
  52.4 4.5 %copy-start.4 = (f32[2048,64]{1,0:T(8,128)S(1)}, f32[2048,64]{1,0:T(8,128)}, u32[]{:S(2)}) copy-start(f32[2048,64]{1,0:T(8,128)} %gather_fusion.4) | copy-start | bytes 1572868
  52.5 4.5 %copy-start.5 = (f32[2048,64]{1,0:T(8,128)S(1)}, f32[2048,64]{1,0:T(8,128)}, u32[]{:S(2)}) copy-start(f32[2048,64]{1,0:T(8,128)} %gather_fusion.3) | copy-start | bytes 1572868
  105.2 19.0 %copy-start.1 = (f32[512,7552]{1,0:T(8,128)S(1)}, f32[512,7552]{1,0:T(8,128)}, u32[]{:S(2)}) copy-start(f32[512,7552]{1,0:T(8,128)} %all-gather.2.cloned.1.call-done) | copy-start | bytes 46399492
  105.2 19.0 %copy-start.2 = (f32[128,7552]{1,0:T(8,128)S(1)}, f32[128,7552]{1,0:T(8,128)}, u32[]{:S(2)}) copy-start(f32[128,7552]{1,0:T(8,128)} %param.14) | copy-start | bytes 11599876
  124.2 17.2 %copy-start.10 = (u32[256]{0:T(256)S(1)}, u32[256]{0:T(256)}, u32[]{:S(2)}) copy-start(u32[256]{0:T(256)} %constant.114) | copy-start | bytes 3076
  124.3 18.6 %copy-start.9 = (s32[64]{0:T(128)S(1)}, s32[64]{0:T(128)}, u32[]{:S(2)}) copy-start(s32[64]{0:T(128)} %param.18) | copy-start | bytes 772
  271.4 94.9 %copy-start.6 = (f32[128,2048]{0,1:T(8,128)S(1)}, f32[128,2048]{0,1:T(8,128)}, u32[]{:S(2)}) copy-start(f32[128,2048]{0,1:T(8,128)} %get-tuple-element.128) | copy-start | bytes 3145732
Sparse Core Ops, SparseCore 0:
  9.2 95.9 all-gather.1
  141.6 129.7 all-reduce.3
where the time goes:
time: 397 us; the launch traced here: 396 us
  waiting for transfers between devices  175 us (44%)
  blocking collectives  90.7 us (23%)
  local copies, waits for them, and re-layouts  49.2 us (12%)
  matrix products  36.2 us (9%)
  other arithmetic  30.6 us (8%)
  between operations  14.3 us (4%)
    psum x1, waiting for transfers between devices, on_device(): summed_flows = lax.psum(partial_flows, 'bus')  129 us
    unnamed x1, blocking collectives  54.3 us
    all_gather x1, waiting for transfers between devices, on_device(): piece = lax.all_gather(injections, 'branch', axis=0, tiled=True)  45.4 us
    all_gather x1, blocking collectives, on_device(): lax.all_gather(base_out, 'branch', axis=1, tiled=True)  36.4 us
    reduce_max x8, other arithmetic, advance(): return jnp.maximum(worst_load, jnp.max(jnp.abs(after_outage), axis=1))  21 us
    gather x2, local copies, waits for them, and re-layouts, columns(): jnp.take(matrix, from_index, axis=1) * from_inside[None, :]  19.6 us
    dot_general x1, matrix products, on_device(): lax.dot_general(piece, ptdf_out, contract, precision=highest, preferred_e...  19 us
    gather x2, local copies, waits for them, and re-layouts, columns(): jnp.take(matrix, to_index, axis=1) * to_inside[None, :]  17.3 us
  transfers between devices with their start and end apart: 2, of which 2 were waited for; matrix products, arithmetic and copies ran while one was open for 13% of the time, Pallas kernels for 0%

commit v1 on v0

--- a/solution.py
+++ b/solution.py
@@ -25,7 +25,9 @@
     bus_count = lax.axis_size("bus")
     bus_index = lax.axis_index("bus")
     contract = (((1,), (1,)), ((), ()))
-    piece = lax.all_gather(injections, "branch", axis=0, tiled=True)
+    piece = jnp.concatenate(
+        lax.all_to_all(jnp.stack([injections] * lax.axis_size("branch")), "branch", 0, 0), axis=0
+    )
     monitored = lax.dot_general(
         piece, ptdf_mon, contract, precision=highest, preferred_element_type=jnp.float32
     )

time: 397 us -> 652 us (1.64)
  waiting for transfers between devices: 175 us -> 410 us
  starting transfers between devices: 0.04 us -> 10.2 us
  local copies, waits for them, and re-layouts: 49.2 us -> 56.3 us
    all_to_all x0 -> x1, waiting for transfers between devices: none -> 284 us  [on_device(): lax.all_to_all(jnp.stack([injections] * lax.axis_size('branch')), 'branch...]
    all_gather x1 -> x0, waiting for transfers between devices: 45.4 us -> none  [on_device(): piece = lax.all_gather(injections, 'branch', axis=0, tiled=True)]
    all_to_all x0 -> x1, starting transfers between devices: none -> 10.1 us  [on_device(): lax.all_to_all(jnp.stack([injections] * lax.axis_size('branch')), 'branch...]
    another operation x0 -> x1, local copies, waits for them, and re-layouts: none -> 7.47 us  [on_device(): jnp.stack([injections] * lax.axis_size('branch'))]
  transfers between devices with their start and end apart: 2 -> 2, of which waited for: 2 -> 2; matrix products, arithmetic and copies ran while one was open for 13% -> 8% of each run, Pallas kernels for 0% -> 0%
where the time goes in v1:
time: 652 us; the launch traced here: 651 us
  waiting for transfers between devices  410 us (63%)
  blocking collectives  90.7 us (14%)
  local copies, waits for them, and re-layouts  56.3 us (9%)
  matrix products  36.2 us (6%)
  other arithmetic  33.2 us (5%)
  between operations  14.3 us (2%)
  starting transfers between devices  10.2 us (2%)
    all_to_all x1, waiting for transfers between devices, on_device(): lax.all_to_all(jnp.stack([injections] * lax.axis_size('branch')), 'branch...  284 us
    psum x1, waiting for transfers between devices, on_device(): summed_flows = lax.psum(partial_flows, 'bus')  125 us
    unnamed x1, blocking collectives  54.3 us
    all_gather x1, blocking collectives, on_device(): lax.all_gather(base_out, 'branch', axis=1, tiled=True)  36.4 us
    reduce_max x8, other arithmetic, advance(): return jnp.maximum(worst_load, jnp.max(jnp.abs(after_outage), axis=1))  21 us
    gather x2, local copies, waits for them, and re-layouts, columns(): jnp.take(matrix, from_index, axis=1) * from_inside[None, :]  19.3 us
    dot_general x1, matrix products, on_device(): lax.dot_general(piece, ptdf_mon, contract, precision=highest, preferred_e...  18 us
    gather x2, local copies, waits for them, and re-layouts, columns(): jnp.take(matrix, to_index, axis=1) * to_inside[None, :]  17.4 us
  transfers between devices with their start and end apart: 2, of which 2 were waited for; matrix products, arithmetic and copies ran while one was open for 8% of the time, Pallas kernels for 0%

profile of v1, /device:TPU:6, one launch (start us, length us, event | category | flops | bytes accessed | tf_op | source)
XLA Modules:
  0.0 650.9 jit_solution(11225687527241459590)
XLA Ops:
  6.5 7.5 %stack.2 = f32[32,16,7552]{2,1,0:T(8,128)} broadcast(f32[16,7552]{1,0:T(8,128)} %param.13), dimensions={1,2} | broadcast | bytes 15949824 | tf_op jit(solution)/shard_map/stack | solution.py:29
  14.0 10.1 %all-to-all-start = ((f32[32,16,7552]{2,1,0:T(8,128)}), f32[32,16,7552]{2,1,0:T(8,128)}, u32[]{:S(2)}, u32[]{:S(2)}) async-start(f32[32,16,7552]{2,1,0:T(8,128)} %stack.2), calls=%async_computation | async-start | bytes 30932992 | tf_op jit(solution)/shard_map/all_to_all | solution.py:29
  24.2 5.4 copy.22
  29.6 7.7 %gather_fusion.2 = f32[2048,128]{1,0:T(8,128)S(1)} fusion(f32[128,7552]{0,1:T(8,128)} %copy.22, s32[2048]{0:T(1024)S(1)} %get-tuple-element.139), kind=kCustom, calls=%fused_computation.2.clone | custom fusion | bytes 2105344 | tf_op jit(solution)/shard_map/jit(_take)/gather | solution.py:54
  37.3 9.7 %gather_fusion.1 = f32[2048,128]{1,0:T(8,128)} fusion(f32[128,7552]{0,1:T(8,128)} %copy.22, s32[2048]{0:T(1024)S(1)} %get-tuple-element.138), kind=kCustom, calls=%fused_computation.clone | custom fusion | bytes 2105344 | tf_op jit(solution)/shard_map/jit(_take)/gather | solution.py:53
  47.0 2.6 copy.24
  49.6 9.7 %gather_fusion.4 = f32[2048,64]{1,0:T(8,128)} fusion(f32[64,7552]{0,1:T(8,128)} %copy.24, s32[2048]{0:T(1024)S(1)} %get-tuple-element.139), kind=kCustom, calls=%fused_computation.3.clone | custom fusion | bytes 1056768 | tf_op jit(solution)/shard_map/jit(_take)/gather | solution.py:54
  59.3 9.7 %gather_fusion.3 = f32[2048,64]{1,0:T(8,128)} fusion(f32[64,7552]{0,1:T(8,128)} %copy.24, s32[2048]{0:T(1024)S(1)} %get-tuple-element.138), kind=kCustom, calls=%fused_computation.1.clone | custom fusion | bytes 1056768 | tf_op jit(solution)/shard_map/jit(_take)/gather | solution.py:53
  69.0 4.3 fusion.1
  73.3 4.5 fusion
  77.7 284.4 %all-to-all-done = f32[32,16,7552]{2,1,0:T(8,128)} async-done(((f32[32,16,7552]{2,1,0:T(8,128)}), f32[32,16,7552]{2,1,0:T(8,128)}, u32[]{:S(2)}, u32[]{:S(2)}) %all-to-all-start) | async-done | bytes 15466528 | tf_op jit(solution)/shard_map/all_to_all | solution.py:29
  362.2 17.3 %fusion.7 = f32[512,64]{0,1:T(8,128)S(1)} fusion(f32[512,7552]{1,0:T(8,128)} %bitcast, f32[64,7552]{1,0:T(8,128)S(1)} %copy-done.2), kind=kOutput, calls=%fused_computation.34 | convolution fusion | flops 2969567232 | bytes 17530880 | tf_op jit(solution)/shard_map/dot_general | solution.py:34
  379.5 18.0 %fusion.6 = f32[512,128]{0,1:T(8,128)S(1)} fusion(f32[512,7552]{1,0:T(8,128)} %bitcast, f32[128,7552]{1,0:T(8,128)S(1)} %copy-done.1), kind=kOutput, calls=%fused_computation.33 | convolution fusion | flops 5939134464 | bytes 19595264 | tf_op jit(solution)/shard_map/dot_general | solution.py:31
  399.8 125.3 %all-reduce.4.cloned.1.call-done = (f32[512,192]{0,1:T(8,128)}, f32[128,2048]{0,1:T(8,128)}, f32[64,2048]{0,1:T(8,128)}) async-done(((f32[512,192]{0,1:T(8,128)}, f32[128,2048]{0,1:T(8,128)}, f32[64,2048]{0,1:T(8,128)}), (f32[512,192]{0,1:T(8,128)}, f32[128,2048]{0,1:T(8,128)}, f32[64,2048]{0,1:T(8,128)})) %all-reduce.4.cloned.1.call-update) | async-done | bytes 1966096 | tf_op jit(solution)/shard_map/psum | solution.py:39
  527.0 36.4 %all_gather.6 = f32[64,2048]{0,1:T(8,128)S(1)} all-gather(f32[64,64]{0,1:T(8,128)S(1)} %dynamic-slice.2), channel_id=1, replica_groups=mesh['branch'=32,'bus'=8] {'branch'}, dimensions={1}, use_global_device_ids=true | all-gather | bytes 540672 | tf_op jit(solution)/shard_map/all_gather | solution.py:63
  565.6 54.3 %all-reduce = f32[2048]{0:T(1024)S(1)} all-reduce(f32[2048]{0:T(1024)S(1)} %dynamic-update-slice), channel_id=1, replica_groups=mesh['branch'=32,'bus'=8] {'branch'}, use_global_device_ids=true, to_apply=%add | all-reduce | flops 2048 | bytes 16384
  621.5 21.7 %while.13 = (s32[]{:T(128)}, f32[64,128]{1,0:T(8,128)S(1)}, f32[64,128]{1,0:T(8,128)S(1)}, f32[64,2048]{1,0:T(8,128)S(1)}, f32[2048,128]{1,0:T(8,128)S(1)}, /*index=5*/s32[]{:T(128)}, s32[]{:T(128)}, s32[]{:T(128)}, s32[]{:T(128)}) while((s32[]{:T(128)}, f32[64,128]{1,0:T(8,128)S(1)}, f32[64,128]{1,0:T(8,128)S(1)}, f32[64,2048]{1,0:T(8,128)S(1)}, ...), condition=%wide.region_5.8_spmd, body=%wide.region_3.7_spmd.sunk | while | flops 8388614 | bytes 753819 | solution.py:17
  621.6 2.6 abs_reduce_fusion.2
  624.3 2.6 abs_reduce_fusion.2
  627.0 2.6 abs_reduce_fusion.2
  629.7 2.6 abs_reduce_fusion.2
  632.4 2.6 abs_reduce_fusion.2
  635.2 2.6 abs_reduce_fusion.2
  637.9 2.6 abs_reduce_fusion.2
  (59 shorter events, 11.0 us)
Async XLA Ops:
  6.5 636.7 %copy-start = (f32[128,4]{0,1:T(4,128)S(1)}, f32[128,4]{0,1:T(4,128)}, u32[]{:S(2)}) copy-start(f32[128,4]{0,1:T(4,128)} %param.19) | copy-start | bytes 6148
  14.0 15.6 %copy-start.3 = (s32[2048]{0:T(1024)S(1)}, s32[2048]{0:T(1024)}, u32[]{:S(2)}) copy-start(s32[2048]{0:T(1024)} %param.16) | copy-start | bytes 24580
  14.0 15.6 %copy-start.4 = (s32[2048]{0:T(1024)S(1)}, s32[2048]{0:T(1024)}, u32[]{:S(2)}) copy-start(s32[2048]{0:T(1024)} %param.17) | copy-start | bytes 24580
  14.0 348.2 %all-to-all-start = ((f32[32,16,7552]{2,1,0:T(8,128)}), f32[32,16,7552]{2,1,0:T(8,128)}, u32[]{:S(2)}, u32[]{:S(2)}) async-start(f32[32,16,7552]{2,1,0:T(8,128)} %stack.2), calls=%async_computation | async-start | bytes 30932992 | tf_op jit(solution)/shard_map/all_to_all | solution.py:29
  24.1 501.0 %all-reduce.4.cloned.1.call-start = ((), (), s32[]{:S(2)}) async-start(), calls=%async_computation.1 | async-start | bytes 4980736 | tf_op jit(solution)/shard_map/psum | solution.py:39
  29.6 17.4 %copy-start.2 = (f32[64,7552]{1,0:T(8,128)S(1)}, f32[64,7552]{1,0:T(8,128)}, u32[]{:S(2)}) copy-start(f32[64,7552]{1,0:T(8,128)} %param.15) | copy-start | bytes 5799940
  362.2 17.3 %copy-start.1 = (f32[128,7552]{1,0:T(8,128)S(1)}, f32[128,7552]{1,0:T(8,128)}, u32[]{:S(2)}) copy-start(f32[128,7552]{1,0:T(8,128)} %param.14) | copy-start | bytes 11599876
  379.5 18.9 %copy-start.6 = (u32[256]{0:T(256)S(1)}, u32[256]{0:T(256)}, u32[]{:S(2)}) copy-start(u32[256]{0:T(256)} %constant.114) | copy-start | bytes 3076
  379.5 20.2 %copy-start.5 = (s32[64]{0:T(128)S(1)}, s32[64]{0:T(128)}, u32[]{:S(2)}) copy-start(s32[64]{0:T(128)} %param.18) | copy-start | bytes 772
Sparse Core Ops, SparseCore 0:
  398.5 126.5 all-reduce.3
